TPU v7x, 512 devices: a whole 4x8x8 slice. The times are simulated.
512 devices in a mesh: layer: 16 (over z, core), ex: 32 (over y, x).
Axes of the slice: x: 4, y: 8, z: 8, core: 2. Of those that a mesh axis runs over, the one named last changes fastest.
Arguments:
- train_grads: bfloat16 [16384, 16, 4096], P('ex', 'layer'), may hold values from -0.3984375 to 0.3984375
- query_grads: bfloat16 [2048, 16, 4096], P('ex', 'layer'), may hold values from -0.3984375 to 0.3984375
- in_precond: float32 [16, 64, 64], P('layer'), as said below
- out_precond: float32 [16, 64, 64], P('layer'), as said below
- pair_blocks: int32 [768], replicated, may hold values from -1 to 127, as said below
Outputs:
- tile_out: float32 [16, 768, 512], P('layer', 'ex')
Inputs may be any that keep to these rules, and one draw needn't show every extreme that they name: `pair_blocks`: slots p of training block p // 24 name query blocks (query block q holds judged examples q * 16 to q * 16 + 15 and lies on ex index q // 4), or -1 for an empty slot; the blocks named by one training block lie on distinct ex indices; empty slots come after filled ones; every training block fills at least 6 slots and some training block fills all 24. `in_precond`: each layer's factor is symmetric positive definite. `out_precond`: each layer's factor is symmetric positive definite.
All inputs are finite; a program needn't handle non-finite values.
Results may differ from a plain program's by a relative error of at most 0.0029.
Values may be sent and summed in bfloat16 or wider, within the bound.
A program may use at most 64 MiB of HBM per device.

v0:
```python
import jax
import jax.numpy as jnp
from jax import lax
from jax.sharding import PartitionSpec as P

QBLK = 16


def precondition(blocks, in_precond, out_precond):
    leading = blocks.shape[:-2]
    layers = blocks.shape[-2]
    out_width = out_precond.shape[-1]
    in_width = in_precond.shape[-1]
    matrices = blocks.astype(jnp.float32).reshape((-1, layers, out_width, in_width))
    left_side = jnp.einsum("loj,rlji->rloi", out_precond, matrices, precision=lax.Precision.HIGHEST)
    precond = jnp.einsum("rloi,lik->rlok", left_side, in_precond, precision=lax.Precision.HIGHEST)
    return precond.reshape(leading + (layers, out_width * in_width)).astype(jnp.bfloat16)


def shards(train_grads, query_grads, in_precond, out_precond, pair_blocks):
    ex_count = lax.axis_size("ex")
    my_index = lax.axis_index("ex")
    layers = train_grads.shape[1]
    features = train_grads.shape[2]
    held_blocks = query_grads.shape[0] // QBLK
    slot_count = pair_blocks.shape[0] // ex_count
    wanted = pair_blocks.reshape(ex_count, slot_count)
    holder = jnp.where(wanted >= 0, wanted // held_blocks, -1)
    local_block = wanted - my_index * held_blocks
    matches = (holder == my_index)[:, :, None] & (
        local_block[:, :, None] == jnp.arange(held_blocks)[None, None, :]
    )
    picker = jnp.any(matches, axis=1).astype(jnp.bfloat16)
    blocks = query_grads.reshape(held_blocks, QBLK, layers, features)
    blocks = precondition(blocks, in_precond, out_precond)
    outgoing = jnp.einsum(
        "dk,kalf->dalf", picker, blocks, preferred_element_type=jnp.float32
    ).astype(jnp.bfloat16)
    received = lax.all_to_all(outgoing, "ex", split_axis=0, concat_axis=0, tiled=True)
    own_slots = lax.dynamic_slice_in_dim(pair_blocks, my_index * slot_count, slot_count, 0)
    source = jnp.where(own_slots >= 0, own_slots // held_blocks, -1)
    chooser = (source[:, None] == jnp.arange(ex_count)[None, :]).astype(jnp.bfloat16)
    chosen = jnp.einsum(
        "sn,nalf->salf", chooser, received, preferred_element_type=jnp.float32
    ).astype(jnp.bfloat16)
    return lax.psum_scatter(
        jnp.einsum("salf,rlf->asr", chosen, train_grads, preferred_element_type=jnp.float32),
        "layer",
        scatter_dimension=0,
        tiled=True,
    )


def solution(mesh):
    in_specs = (
        P("ex", "layer", None),
        P("ex", "layer", None),
        P("layer", None, None),
        P("layer", None, None),
        P(),
    )
    out_specs = P("layer", "ex", None)
    return jax.shard_map(shards, mesh=mesh, in_specs=in_specs, out_specs=out_specs, check_vma=False)
```

profile of v0, /device:TPU:1, one launch (start us, length us, event | category | flops | bytes accessed | tf_op | source)
XLA Modules:
  0.0 204.0 jit_solution(126892212329123031)
XLA Ops:
  6.5 0.0 copy-start
  6.5 0.0 copy-start.1
  6.5 0.8 reshape.81
  7.3 0.1 copy.28
  7.4 0.1 copy.33
  7.5 2.1 %reshape.82 = bf16[64,64,64]{2,1,0:T(8,128)(2,1)S(1)} reshape(bf16[64,1,4096]{2,0,1:T(8,128)(2,1)} %param.6) | data formatting | bytes 1048576 | tf_op jit(solution)/shard_map/reshape.1
  9.6 0.0 copy-done
  9.6 1.2 fusion.24
  10.8 0.0 copy-done.1
  10.8 3.5 %fusion.12 = bf16[64,1,64,64]{3,2,0,1:T(8,128)(2,1)S(1)} fusion(f32[64,64,64]{2,1,0:T(8,128)S(1)} %fusion.24, f32[1,64,64]{2,1,0:T(8,128)S(1)} %copy-done.1), kind=kOutput, calls=%fused_computation.10 | convolution fusion | flops 201588736 | bytes 1589248 | tf_op jit(solution)/shard_map/rloi,lik->rlok/dot_general | solution.py:16
  14.4 0.8 convert_element_type.35
  15.2 1.3 fusion
  16.5 4.3 %copy.37 = bf16[32,16,1,4096]{3,1,2,0:T(8,128)(2,1)} copy(bf16[32,16,1,4096]{3,0,1,2:T(8,128)(2,1)S(1)} %fusion) | data formatting | bytes 8388608 | tf_op jit(solution)/shard_map/convert_element_type | solution.py:38
  20.8 10.6 %all-to-all-start = ((bf16[32,16,1,4096]{3,1,2,0:T(8,128)(2,1)}), bf16[32,16,1,4096]{3,1,2,0:T(8,128)(2,1)}, u32[]{:S(2)}, u32[]{:S(2)}) async-start(bf16[32,16,1,4096]{3,1,2,0:T(8,128)(2,1)} %copy.37), calls=%async_computation | async-start | bytes 8388608 | tf_op jit(solution)/shard_map/all_to_all | solution.py:39
  31.4 0.2 reduce-scatter.2.cloned.1.call-start
  31.6 0.8 compare_select_fusion
  32.4 91.6 %all-to-all-done = bf16[32,16,1,4096]{3,1,2,0:T(8,128)(2,1)} async-done(((bf16[32,16,1,4096]{3,1,2,0:T(8,128)(2,1)}), bf16[32,16,1,4096]{3,1,2,0:T(8,128)(2,1)}, u32[]{:S(2)}, u32[]{:S(2)}) %all-to-all-start) | async-done | bytes 4194336 | tf_op jit(solution)/shard_map/all_to_all | solution.py:39
  124.1 10.8 %fusion.15 = f32[16,24,512]{2,1,0:T(8,128)} fusion(bf16[512,1,4096]{2,0,1:T(8,128)(2,1)} %param.5, bf16[32,16,1,4096]{3,1,2,0:T(8,128)(2,1)} %all-to-all-done, s32[24]{0:T(128)S(1)} %compare_select_fusion), kind=kOutput, calls=%fused_computation.11 | convolution fusion | flops 1712849664 | bytes 9175136 | tf_op jit(solution)/shard_map/salf,rlf->asr/dot_general | solution.py:47
  134.9 0.0 reduce-scatter.2.cloned.1.call-update
  134.9 62.3 %reduce-scatter.2.cloned.1.call-done = f32[1,24,512]{2,1,0:T(8,128)} async-done(((f32[16,24,512]{2,1,0:T(8,128)}), f32[1,24,512]{2,1,0:T(8,128)}) %reduce-scatter.2.cloned.1.call-update) | async-done | bytes 49168 | tf_op jit(solution)/shard_map/reduce_scatter | solution.py:46
  (3 shorter events, 0.1 us)
Async XLA Ops:
  6.5 3.0 %copy-start = (f32[1,64,64]{2,1,0:T(8,128)S(1)}, f32[1,64,64]{2,1,0:T(8,128)}, u32[]{:S(2)}) copy-start(f32[1,64,64]{2,1,0:T(8,128)} %param.8) | copy-start | bytes 49156
  6.5 4.3 %copy-start.1 = (f32[1,64,64]{2,1,0:T(8,128)S(1)}, f32[1,64,64]{2,1,0:T(8,128)}, u32[]{:S(2)}) copy-start(f32[1,64,64]{2,1,0:T(8,128)} %param.7) | copy-start | bytes 49156
  20.8 103.3 %all-to-all-start = ((bf16[32,16,1,4096]{3,1,2,0:T(8,128)(2,1)}), bf16[32,16,1,4096]{3,1,2,0:T(8,128)(2,1)}, u32[]{:S(2)}, u32[]{:S(2)}) async-start(bf16[32,16,1,4096]{3,1,2,0:T(8,128)(2,1)} %copy.37), calls=%async_computation | async-start | bytes 8388608 | tf_op jit(solution)/shard_map/all_to_all | solution.py:39
  31.4 165.8 %reduce-scatter.2.cloned.1.call-start = ((), (), s32[]{:S(2)}) async-start(), calls=%async_computation.2 | async-start | bytes 835584 | tf_op jit(solution)/shard_map/reduce_scatter | solution.py:46
Sparse Core Ops, SparseCore 0:
  135.0 62.1 reduce-scatter.1
where the time goes:
time: 206 us; the launch traced here: 204 us
  waiting for transfers between devices  154 us (75%)
  matrix products  16.9 us (8%)
  between operations  13.5 us (7%)
  starting transfers between devices  10.8 us (5%)
  local copies, waits for them, and re-layouts  8.04 us (4%)
    all_to_all x1, waiting for transfers between devices, shards(): lax.all_to_all(outgoing, 'ex', split_axis=0, concat_axis=0, tiled=True)  91.6 us
    reduce_scatter x1, waiting for transfers between devices, shards(): lax.psum_scatter(jnp.einsum('salf,rlf->asr', chosen, train_grads, preferr...  62.3 us
    dot_general x1, matrix products, shards(): jnp.einsum('salf,rlf->asr', chosen, train_grads, preferred_element_type=j...  10.8 us
    all_to_all x1, starting transfers between devices, shards(): lax.all_to_all(outgoing, 'ex', split_axis=0, concat_axis=0, tiled=True)  10.6 us
    convert_element_type x1, local copies, waits for them, and re-layouts, shards(): outgoing = jnp.einsum('dk,kalf->dalf', picker, blocks, preferred_element_...  4.26 us
  transfers between devices with their start and end apart: 2, of which 2 were waited for; matrix products, arithmetic and copies ran while one was open for 0% of the time, Pallas kernels for 0%

commit v1 on v0

v1 whole, which is shorter than its diff:
```python
import functools

import jax
import jax.numpy as jnp
from jax import lax
from jax.experimental import pallas as pl
from jax.experimental.pallas import tpu as pltpu
from jax.sharding import PartitionSpec as P

MESH = pl.DeviceIdType.MESH
NX = 4
HELD = 4
NC = 4
LANES = 128
LAG = 3


def precondition(blocks, in_precond, out_precond):
    matrices = blocks.astype(jnp.float32).reshape((-1, out_precond.shape[-1], in_precond.shape[-1]))
    left_side = jnp.einsum("oj,rji->roi", out_precond, matrices, precision=lax.Precision.HIGHEST)
    precond = jnp.einsum("roi,ik->rok", left_side, in_precond, precision=lax.Precision.HIGHEST)
    return precond.reshape(matrices.shape[0], -1).astype(jnp.bfloat16)


def kernel(
    n_ex, layers, slots,
    pick_ref, pair_ref, own_hbm, train_hbm, out_ref,
    ag, recv, stage, fwd, train_v, acc, send_pair, recv_pair, send_one, recv_one, total,
    load_sem, ag_send, ag_recv, x_send, x_recv, fwd_send, fwd_recv, pair_send, one_send, pair_recv, one_recv,
):
    ny = n_ex // NX
    half = ny // 2
    cuts = acc.shape[0]
    rows = layers
    regular = NC * (half - 1)
    items = regular + NC // 2
    last = ny - 1
    ex = lax.axis_index("ex")
    lay = lax.axis_index("layer")
    y, x = ex // NX, ex % NX
    up = ((y + 1) % ny) * NX + x
    down = ((y + ny - 1) % ny) * NX + x
    right = y * NX + (x + 1) % NX
    left = y * NX + (x + NX - 1) % NX
    across = y * NX + (x + 2) % NX

    def load_own():
        return pltpu.make_async_copy(own_hbm, ag.at[pl.ds(0, NC)], load_sem.at[NC])

    def load_train(c):
        width = train_v.shape[2]
        return pltpu.make_async_copy(train_hbm.at[:, pl.ds(c * width, width)], train_v.at[c], load_sem.at[c])

    load_own().start()
    for c in range(NC):
        load_train(c).start()

    barrier = pltpu.get_barrier_semaphore()
    for peer in (up, down, right, left):
        pl.semaphore_signal(barrier, inc=1, device_id={"ex": peer}, device_id_type=MESH)

    @pl.loop(1, layers)
    def _(r):
        pl.semaphore_signal(barrier, inc=1, device_id={"layer": (lay + r) % layers}, device_id_type=MESH)

    acc[...] = jnp.zeros_like(acc)
    load_own().wait()
    pl.semaphore_wait(barrier, 4 + layers - 1)

    def send_along(src, dst, sem, peer):
        pltpu.make_async_remote_copy(
            src_ref=ag.at[src], dst_ref=ag.at[dst], send_sem=ag_send, recv_sem=ag_recv.at[sem],
            device_id={"ex": peer}, device_id_type=MESH,
        ).start()

    def plus(src, m):
        send_along(src, NC + m, m, up)

    def minus(src, m):
        send_along(src, NC + items + m, items + m, down)

    def wait_along(m):
        for side in range(2):
            there = ag.at[NC + side * items + m]
            pltpu.make_async_copy(there, there, ag_recv.at[side * items + m]).wait()

    for c in range(NC):
        plus(c, c)
        minus(c, c)

    def choose(src, label, c, row):
        blocks = [ag[src, pl.ds(b * rows, rows), :] for b in range(HELD)]
        for j, to in enumerate((ex, right, left, across)):
            want = pick_ref[to * n_ex + row * NX + x]
            v = blocks[HELD - 1]
            for b in range(HELD - 1):
                v = jnp.where(want == b, blocks[b], v)
            if j == 0:
                recv[c, label, pl.ds(0, rows), :] = v
            else:
                stage[c, label, j - 1] = v

    def push(label, c, via):
        def one(j, dst, sem, peer):
            pltpu.make_async_remote_copy(
                src_ref=stage.at[c, label, j], dst_ref=dst, send_sem=x_send, recv_sem=sem,
                device_id={"ex": peer}, device_id_type=MESH,
            ).start()

        one(2, fwd.at[c, label], fwd_recv.at[c, label], via)
        one(0, recv.at[c, label, pl.ds(rows, rows)], x_recv.at[c, label], right)
        one(1, recv.at[c, label, pl.ds(2 * rows, rows)], x_recv.at[c, label], left)

    def relay(label, c, via):
        here = fwd.at[c, label]
        pltpu.make_async_copy(here, here, fwd_recv.at[c, label]).wait()
        pltpu.make_async_remote_copy(
            src_ref=here, dst_ref=recv.at[c, label, pl.ds(3 * rows, rows)], send_sem=fwd_send,
            recv_sem=x_recv.at[c, label], device_id={"ex": via}, device_id_type=MESH,
        ).start()

    def arrived(label, c):
        there = recv.at[c, label, pl.ds(rows, 3 * rows)]
        pltpu.make_async_copy(there, there, x_recv.at[c, label]).wait()

    def multiply(label, c, count):
        for i in range(count):
            arrived(label + i, c)
        tall = count * NX * rows
        block = recv[c, pl.ds(label, count)].reshape(tall, recv.shape[3])
        where = pl.ds(pl.multiple_of(label * NX * rows, NX * rows), tall)
        product = lax.dot_general(
            block, train_v[c], (((1,), (1,)), ((), ())), preferred_element_type=jnp.float32
        )
        for n in range(cuts):
            acc[n, where, :] += product[:, n * LANES : (n + 1) * LANES]

    def scatter(src, dst, out_sem, sem):
        @pl.loop(1, layers)
        def _(r):
            to = (lay + r) % layers
            pltpu.make_async_remote_copy(
                src_ref=src.at[to], dst_ref=dst.at[r - 1], send_sem=out_sem, recv_sem=sem,
                device_id={"layer": to}, device_id_type=MESH,
            ).start()

    def reduce_pair(g):
        base = (2 * g + 1) * NX * rows

        for a in range(rows):
            for n in range(cuts):
                v = acc[n, pl.ds(base + a, 2 * NX, stride=rows), :]
                send_pair[g, a, pl.ds(n * 2 * NX, 2 * NX), :] = v
        scatter(send_pair.at[g], recv_pair.at[g], pair_send, pair_recv.at[g])

    def reduce_one(i):
        base = (0 if i == 0 else last) * NX * rows

        for a in range(rows):
            for n in range(cuts):
                v = acc[n, pl.ds(base + a, NX, stride=rows), :]
                send_one[i, a, pl.ds(n * NX, NX), :] = v
        scatter(send_one.at[i], recv_one.at[i], one_send, one_recv.at[i])

    def own_via(c):
        return right if c % 2 == 0 else left

    for c in range(NC):
        choose(c, 0, c, y)
    for c in range(NC):
        push(0, c, own_via(c))

    def labels(m):
        k = m // NC + 1
        return 2 * k - 1, 2 * k, m % NC

    def relay_step(m):
        a, b, c = labels(m)
        relay(a, c, right)
        relay(b, c, left)

    def multiply_step(m):
        a, _, c = labels(m)
        multiply(a, c, 2)

    @pl.loop(0, regular)
    def _(m):
        k = m // NC + 1
        a, b, c = labels(m)
        wait_along(m)

        @pl.when(m < items - NC)
        def _():
            plus(NC + m, m + NC)

        @pl.when((m < regular - NC) | (m >= regular - NC // 2))
        def _():
            minus(NC + items + m, jnp.where(m < regular - NC, m + NC, m + NC // 2))

        choose(NC + m, a, c, (y + ny - k) % ny)
        choose(NC + items + m, b, c, (y + k) % ny)
        push(a, c, right)
        push(b, c, left)

        @pl.when(m == 0)
        def _():
            for i in range(NC):
                relay(0, i, own_via(i))
                load_train(i).wait()

        @pl.when(m > 0)
        def _():
            relay_step(m - 1)

        @pl.when(m == 2)
        def _():
            @pl.loop(0, NC)
            def _(i):
                multiply(0, i, 1)

            reduce_one(0)

        @pl.when(m >= LAG)
        def _():
            multiply_step(m - LAG)

        for g in range(half - 1):
            if NC * g + NC - 1 + LAG < regular:

                @pl.when(m == NC * g + NC - 1 + LAG)
                def _():
                    reduce_pair(g)

    opposite = (y + half) % ny
    spots = [((t, right), (NC // 2 + t, left)) for t in range(NC // 2)]
    for t, spot in enumerate(spots):
        m = regular + t
        wait_along(m)
        for side, (c, _) in enumerate(spot):
            choose(NC + side * items + m, last, c, opposite)
        for c, via in spot:
            push(last, c, via)
        if t == 0:
            relay_step(regular - 1)
        else:
            for c, via in spots[t - 1]:
                relay(last, c, via)
        multiply_step(m - LAG)
    for c, via in spots[-1]:
        relay(last, c, via)
    for m in range(regular + len(spots) - LAG, regular):
        multiply_step(m)
    reduce_pair(half - 2)
    for spot in spots:
        for c, _ in spot:
            multiply(last, c, 1)
    reduce_one(1)

    def take_pair(g):
        there = recv_pair.at[g]
        pltpu.make_async_copy(there, there, pair_recv.at[g]).wait()
        v = send_pair[g, lay]
        for r in range(layers - 1):
            v = v + recv_pair[g, r]
        for n in range(cuts):
            where = pl.ds((2 * g + 1) * NX, 2 * NX)
            total[where, pl.ds(n * LANES, LANES)] = v[n * 2 * NX : (n + 1) * 2 * NX]

    def take_one(i):
        there = recv_one.at[i]
        pltpu.make_async_copy(there, there, one_recv.at[i]).wait()
        v = send_one[i, lay]
        for r in range(layers - 1):
            v = v + recv_one[i, r]
        for n in range(cuts):
            where = pl.ds((0 if i == 0 else last) * NX, NX)
            total[where, pl.ds(n * LANES, LANES)] = v[n * NX : (n + 1) * NX]

    take_one(0)
    for g in range(half - 1):
        take_pair(g)
    take_one(1)

    for p in range(slots):
        block = pair_ref[ex * slots + p]
        source = jnp.maximum(block, 0) // HELD
        dy = (source // NX - y + ny) % ny
        dx = (source % NX - x + NX) % NX
        label = jnp.where(dy == half, last, jnp.where(dy < half, 2 * dy, 2 * (ny - dy) - 1))
        off = jnp.where(dx == 3, 1, jnp.where(dx == 1, 2, jnp.where(dx == 2, 3, 0)))
        v = total[pl.ds(label * NX + off, 1), :]
        out_ref[0, pl.ds(p, 1), :] = jnp.where(block >= 0, v, jnp.zeros_like(v))

    sent = ag.at[pl.ds(NC, 2 * items)]
    pltpu.make_async_copy(sent, sent, ag_send).wait()
    pltpu.make_async_copy(stage, stage, x_send).wait()
    pltpu.make_async_copy(fwd, fwd, fwd_send).wait()
    pltpu.make_async_copy(recv_pair, recv_pair, pair_send).wait()
    pltpu.make_async_copy(recv_one, recv_one, one_send).wait()


def shards(train_grads, query_grads, in_precond, out_precond, pair_blocks):
    n_ex = lax.axis_size("ex")
    layers = lax.axis_size("layer")
    features = train_grads.shape[2]
    width = features // NC
    held_rows = query_grads.shape[0]
    rows = held_rows // HELD
    train_rows = train_grads.shape[0]
    cuts = train_rows // LANES
    slots = pair_blocks.shape[0] // n_ex
    ny = n_ex // NX
    half = ny // 2
    items = NC * (half - 1) + NC // 2

    wanted = pair_blocks.reshape(n_ex, slots)
    hit = (wanted[:, :, None] // HELD == jnp.arange(n_ex)[None, None, :]) & (wanted[:, :, None] >= 0)
    pick = jnp.sum(jnp.where(hit, wanted[:, :, None] % HELD, 0), axis=1).astype(jnp.int32).reshape(-1)

    own = precondition(query_grads[:, 0, :], in_precond[0], out_precond[0])
    own = own.reshape(held_rows, NC, width).transpose(1, 0, 2)
    train = train_grads.reshape(train_rows, features)

    bf16, f32 = jnp.bfloat16, jnp.float32
    dma = pltpu.SemaphoreType.DMA
    return pl.pallas_call(
        functools.partial(kernel, n_ex, layers, slots),
        out_shape=jax.ShapeDtypeStruct((1, slots, train_rows), f32),
        in_specs=[
            pl.BlockSpec(memory_space=pltpu.SMEM),
            pl.BlockSpec(memory_space=pltpu.SMEM),
            pl.BlockSpec(memory_space=pl.ANY),
            pl.BlockSpec(memory_space=pl.ANY),
        ],
        out_specs=pl.BlockSpec(memory_space=pltpu.VMEM),
        scratch_shapes=[
            pltpu.VMEM((NC + 2 * items, held_rows, width), bf16),
            pltpu.VMEM((NC, ny, NX * rows, width), bf16),
            pltpu.VMEM((NC, ny, 3, rows, width), bf16),
            pltpu.VMEM((NC, ny, rows, width), bf16),
            pltpu.VMEM((NC, train_rows, width), bf16),
            pltpu.VMEM((cuts, ny * NX * rows, LANES), f32),
            pltpu.VMEM((half - 1, layers, cuts * 2 * NX, LANES), f32),
            pltpu.VMEM((half - 1, layers - 1, cuts * 2 * NX, LANES), f32),
            pltpu.VMEM((2, layers, cuts * NX, LANES), f32),
            pltpu.VMEM((2, layers - 1, cuts * NX, LANES), f32),
            pltpu.VMEM((ny * NX, train_rows), f32),
            dma((NC + 1,)),
            dma,
            dma((2 * items,)),
            dma,
            dma((NC, ny)),
            dma,
            dma((NC, ny)),
            dma,
            dma,
            dma((half - 1,)),
            dma((2,)),
        ],
        compiler_params=pltpu.CompilerParams(
            collective_id=0, has_side_effects=True, vmem_limit_bytes=48 * 1024 * 1024
        ),
        name="tiles",
    )(pick, pair_blocks, own, train)


def solution(mesh):
    in_specs = (
        P("ex", "layer", None),
        P("ex", "layer", None),
        P("layer", None, None),
        P("layer", None, None),
        P(),
    )
    out_specs = P("layer", "ex", None)
    return jax.shard_map(shards, mesh=mesh, in_specs=in_specs, out_specs=out_specs, check_vma=False)
```

time: 206 us -> 86.4 us (0.42)
  waiting for transfers between devices: 154 us -> 0 us
  Pallas kernels: 0 us -> 74.3 us
  between operations: 13.5 us -> 0.12 us
  matrix products: 16.9 us -> 4.76 us
  starting transfers between devices: 10.8 us -> 0 us
    all_to_all x1 -> x0, waiting for transfers between devices: 91.6 us -> none  [shards(): lax.all_to_all(outgoing, 'ex', split_axis=0, concat_axis=0, tiled=True)]
    pallas_call x0 -> x1, Pallas kernels: none -> 74.3 us  [shards(): pl.pallas_call(functools.partial(kernel, n_ex, layers, slots), out_shape=...]
    reduce_scatter x1 -> x0, waiting for transfers between devices: 62.3 us -> none  [shards(): lax.psum_scatter(jnp.einsum('salf,rlf->asr', chosen, train_grads, preferr...]
    dot_general x4 -> x2, matrix products: 16.9 us -> 4.76 us  [the longest x1 3.52 us: precondition(): jnp.einsum('roi,ik->rok', left_side, in_precond, precision=lax.Precision....]
    all_to_all x1 -> x0, starting transfers between devices: 10.6 us -> none  [shards(): lax.all_to_all(outgoing, 'ex', split_axis=0, concat_axis=0, tiled=True)]
    convert_element_type x2, local copies, waits for them, and re-layouts: 5.07 us -> 0.79 us  [precondition(): return precond.reshape(matrices.shape[0], -1).astype(jnp.bfloat16)]
    unnamed x4 -> x9, local copies, waits for them, and re-layouts: 0.01 us -> 2.82 us
  transfers between devices with their start and end apart: 2 -> 0, of which waited for: 2 -> 0; matrix products, arithmetic and copies ran while one was open for 0% -> 0% of each run, Pallas kernels for 0% -> 0%
where the time goes in v1:
time: 86.4 us; the launch traced here: 86.2 us
  Pallas kernels  74.3 us (86%)
  local copies, waits for them, and re-layouts  6.51 us (8%)
  matrix products  4.76 us (6%)
    pallas_call x1, Pallas kernels, shards(): pl.pallas_call(functools.partial(kernel, n_ex, layers, slots), out_shape=...  74.3 us
    dot_general x1, matrix products, precondition(): jnp.einsum('roi,ik->rok', left_side, in_precond, precision=lax.Precision....  3.52 us
    unnamed x9, local copies, waits for them, and re-layouts  2.82 us
    reshape x1, local copies, waits for them, and re-layouts, precondition(): blocks.astype(jnp.float32)  2.06 us

profile of v1, /device:TPU:1, one launch (start us, length us, event | category | flops | bytes accessed | tf_op | source)
XLA Modules:
  0.0 86.2 jit_solution(6862166270064017106)
XLA Ops:
  0.0 0.0 copy-start
  0.0 0.8 broadcast_in_dim_reshape.2
  0.8 0.5 select_reduce_fusion
  1.3 0.1 reshape.108.pick_ref
  1.4 0.0 copy-start.3
  1.4 2.1 %reshape.109 = bf16[64,64,64]{2,1,0:T(8,128)(2,1)S(1)} reshape(bf16[64,1,4096]{2,0,1:T(8,128)(2,1)} %param.6) | data formatting | bytes 1048576 | tf_op jit(solution)/shard_map/reshape | solution.py:19
  3.4 0.0 copy-done
  3.5 1.2 %fusion.7 = f32[64,64,64]{2,1,0:T(8,128)S(1)} fusion(bf16[64,64,64]{2,1,0:T(8,128)(2,1)S(1)} %reshape.109, f32[1,64,64]{2,1,0:T(8,128)S(1)} %copy-done), kind=kOutput, calls=%fused_computation.8 | convolution fusion | flops 201326592 | bytes 1589248 | tf_op jit(solution)/shard_map/oj,rji->roi/dot_general | solution.py:20
  4.7 0.0 copy-done.3
  4.7 3.5 %fusion.2 = bf16[64,64,64]{2,1,0:T(8,128)(2,1)S(1)} fusion(f32[64,64,64]{2,1,0:T(8,128)S(1)} %fusion.7, f32[1,64,64]{2,1,0:T(8,128)S(1)} %copy-done.3), kind=kOutput, calls=%fused_computation.2 | convolution fusion | flops 201588736 | bytes 1589248 | tf_op jit(solution)/shard_map/roi,ik->rok/dot_general | solution.py:21
  8.2 0.0 copy-start.2
  8.3 0.6 convert_element_type.9
  8.9 0.2 copy.13
  9.1 0.0 copy-done.2
  9.1 0.0 copy-start.1
  9.1 2.2 %copy-done.1 = bf16[512,1,4096]{2,0,1:T(8,128)(2,1)S(1)} copy-done((bf16[512,1,4096]{2,0,1:T(8,128)(2,1)S(1)}, bf16[512,1,4096]{2,0,1:T(8,128)(2,1)}, u32[]{:S(2)}) %copy-start.1) | copy-done | bytes 4194328
  11.3 74.3 %tiles.1 = f32[1,24,512]{2,1,0:T(8,128)S(1)} custom-call(s32[1024]{0:T(1024)S(1)} %reshape.108.pick_ref, s32[768]{0:T(1024)S(1)} %copy-done.2, bf16[4,64,1024]{2,1,0:T(8,128)(2,1)S(1)} %bitcast.21, bf16[512,4096]{1,0:T(8,128)(2,1)S(1)} %bitcast.20), custom_call_target="tpu_custom_call" | custom-call | tf_op jit(solution)/shard_map/tiles/pallas_call | solution.py:326
  85.6 0.6 copy.15
  (2 shorter events, 0.0 us)
Async XLA Ops:
  0.0 3.4 %copy-start = (f32[1,64,64]{2,1,0:T(8,128)S(1)}, f32[1,64,64]{2,1,0:T(8,128)}, u32[]{:S(2)}) copy-start(f32[1,64,64]{2,1,0:T(8,128)} %param.8) | copy-start | bytes 49156
  1.4 3.3 %copy-start.3 = (f32[1,64,64]{2,1,0:T(8,128)S(1)}, f32[1,64,64]{2,1,0:T(8,128)}, u32[]{:S(2)}) copy-start(f32[1,64,64]{2,1,0:T(8,128)} %param.7) | copy-start | bytes 49156
  8.2 0.8 copy-start.2
  9.1 2.2 %copy-start.1 = (bf16[512,1,4096]{2,0,1:T(8,128)(2,1)S(1)}, bf16[512,1,4096]{2,0,1:T(8,128)(2,1)}, u32[]{:S(2)}) copy-start(bf16[512,1,4096]{2,0,1:T(8,128)(2,1)} %param.5) | copy-start | bytes 12582916

commit v2 on v1

--- a/solution.py
+++ b/solution.py
@@ -15,17 +15,123 @@
 LAG = 3
 
 
-def precondition(blocks, in_precond, out_precond):
-    matrices = blocks.astype(jnp.float32).reshape((-1, out_precond.shape[-1], in_precond.shape[-1]))
-    left_side = jnp.einsum("oj,rji->roi", out_precond, matrices, precision=lax.Precision.HIGHEST)
-    precond = jnp.einsum("roi,ik->rok", left_side, in_precond, precision=lax.Precision.HIGHEST)
-    return precond.reshape(matrices.shape[0], -1).astype(jnp.bfloat16)
+def wanted_words(pair_ref, destinations, slots, x):
+    def step(p, words):
+        out = []
+        for word, to in zip(words, destinations):
+            block = pair_ref[to * slots + p]
+            source = jnp.right_shift(block, 2)
+            row = jnp.right_shift(source, 2)
+            mine = (block >= 0) & (jnp.bitwise_and(source, NX - 1) == x)
+            bits = jnp.left_shift(jnp.bitwise_and(block, HELD - 1), 2 * jnp.bitwise_and(row, 15))
+            out.append(word | jnp.where(mine, bits, 0))
+        return tuple(out)
+
+    return lax.fori_loop(0, slots, step, (jnp.int32(0),) * len(destinations))
+
+
+def halves(v):
+    high = v.astype(jnp.bfloat16)
+    return high, (v - high.astype(jnp.float32)).astype(jnp.bfloat16)
+
+
+def one_hot(condition):
+    return jnp.where(condition, 1.0, 0.0).astype(jnp.bfloat16)
+
+
+def exact(a, b):
+    return jnp.dot(a, b, preferred_element_type=jnp.float32)
+
+
+def spread_in(factor):
+    n = factor.shape[0]
+    down = lax.broadcasted_iota(jnp.int32, (2 * n, n), 0)
+    across = lax.broadcasted_iota(jnp.int32, (2 * n, n), 1)
+    below = one_hot(down % n == across)
+    down = lax.broadcasted_iota(jnp.int32, (n, 2 * n), 0)
+    across = lax.broadcasted_iota(jnp.int32, (n, 2 * n), 1)
+    beside = one_hot(across % n == down)
+    down = lax.broadcasted_iota(jnp.int32, (2 * n, 2 * n), 0)
+    across = lax.broadcasted_iota(jnp.int32, (2 * n, 2 * n), 1)
+    same = down // n == across // n
+    out = []
+    for half in halves(factor):
+        full = exact(exact(below, half).astype(jnp.bfloat16), beside)
+        out.append(jnp.where(same, full, 0.0).astype(jnp.bfloat16))
+    return jnp.concatenate(out, axis=0)
+
+
+def spread_out(factor):
+    n = factor.shape[0]
+    high, low = halves(factor)
+    down = lax.broadcasted_iota(jnp.int32, (n, n), 0)
+    across = lax.broadcasted_iota(jnp.int32, (n, n), 1)
+    order = one_hot(across == 2 * (down % (n // 2)) + down // (n // 2))
+    down = lax.broadcasted_iota(jnp.int32, (n, 3 * n), 0)
+    across = lax.broadcasted_iota(jnp.int32, (n, 3 * n), 1)
+    inner = across % n
+    hit = down == 2 * (inner % (n // 2)) + inner // (n // 2)
+    first = one_hot(hit & (across < 2 * n))
+    second = one_hot(hit & (across >= 2 * n))
+    high = exact(exact(order, high).astype(jnp.bfloat16), first)
+    low = exact(exact(order, low).astype(jnp.bfloat16), second)
+    return (high + low).astype(jnp.bfloat16)
+
+
+def prepare(query_v, left_factor, right_factor, mid):
+    held, features = query_v.shape
+    pairs = features // LANES
+    n = LANES // 2
+    lane = lax.broadcasted_iota(jnp.int32, (pairs, LANES), 1)
+    low = lane < n
+
+    for d in range(pairs):
+        g = query_v[:, d * LANES : (d + 1) * LANES]
+        both = jnp.concatenate([g, g], axis=1)
+        mid[pl.ds(d * held, held), :] = exact(both, right_factor)
+
+    def side_by_side(t):
+        u0 = mid[pl.ds(2 * t, pairs, stride=held), :]
+        u1 = mid[pl.ds(2 * t + 1, pairs, stride=held), :]
+        even = jnp.where(low, u0, pltpu.roll(u1, n, 1))
+        odd = jnp.where(low, pltpu.roll(u0, n, 1), u1)
+        return halves(jnp.concatenate([even, odd], axis=0))
+
+    def apart(t, z):
+        even, odd = z[:pairs], z[pairs:]
+        mid[pl.ds(2 * t, pairs, stride=held), :] = jnp.where(low, even, pltpu.roll(odd, n, 1))
+        mid[pl.ds(2 * t + 1, pairs, stride=held), :] = jnp.where(low, pltpu.roll(even, n, 1), odd)
+
+    for t in range(0, held // 2, 2):
+        (h0, l0), (h1, l1) = side_by_side(t), side_by_side(t + 1)
+        high = jnp.concatenate([h0, h1], axis=1)
+        rest = jnp.concatenate([l0, l1], axis=1)
+        z = exact(left_factor, jnp.concatenate([high, rest, high], axis=0))
+        apart(t, z[:, :LANES])
+        apart(t + 1, z[:, LANES:])
+
+
+def finish(mid, own):
+    chunks, held, width = own.shape
+    each = width // LANES
+    for d in range(chunks * each):
+        own[d // each, :, pl.ds(d % each * LANES, LANES)] = mid[pl.ds(d * held, held), :].astype(jnp.bfloat16)
+
+
+def prepare_kernel(n_ex, slots, pair_ref, query_ref, in_ref, out_pre_ref, own_ref, words_ref, mid):
+    ex = lax.axis_index("ex")
+    y, x = ex // NX, ex % NX
+    to = [y * NX + (x + d) % NX for d in (0, 1, 3, 2)]
+    for j, word in enumerate(wanted_words(pair_ref, to, slots, x)):
+        words_ref[j] = word
+    prepare(query_ref, spread_out(out_pre_ref[0]), spread_in(in_ref[0]), mid)
+    finish(mid, own_ref)
 
 
 def kernel(
     n_ex, layers, slots,
-    pick_ref, pair_ref, own_hbm, train_hbm, out_ref,
-    ag, recv, stage, fwd, train_v, acc, send_pair, recv_pair, send_one, recv_one, total,
+    words_ref, pair_ref, own_hbm, train_hbm, out_ref,
+    own, ag, recv, stage, fwd, train_v, acc, send_pair, recv_pair, send_one, recv_one, total,
     load_sem, ag_send, ag_recv, x_send, x_recv, fwd_send, fwd_recv, pair_send, one_send, pair_recv, one_recv,
 ):
     ny = n_ex // NX
@@ -45,7 +151,7 @@
     across = y * NX + (x + 2) % NX
 
     def load_own():
-        return pltpu.make_async_copy(own_hbm, ag.at[pl.ds(0, NC)], load_sem.at[NC])
+        return pltpu.make_async_copy(own_hbm, own, load_sem.at[NC])
 
     def load_train(c):
         width = train_v.shape[2]
@@ -66,32 +172,33 @@
     acc[...] = jnp.zeros_like(acc)
     load_own().wait()
     pl.semaphore_wait(barrier, 4 + layers - 1)
-
-    def send_along(src, dst, sem, peer):
+    words = [words_ref[j] for j in range(NX)]
+
+    def send_along(src, dst, peer):
         pltpu.make_async_remote_copy(
-            src_ref=ag.at[src], dst_ref=ag.at[dst], send_sem=ag_send, recv_sem=ag_recv.at[sem],
+            src_ref=src, dst_ref=ag.at[dst], send_sem=ag_send, recv_sem=ag_recv.at[dst],
             device_id={"ex": peer}, device_id_type=MESH,
         ).start()
 
     def plus(src, m):
-        send_along(src, NC + m, m, up)
+        send_along(src, m, up)
 
     def minus(src, m):
-        send_along(src, NC + items + m, items + m, down)
+        send_along(src, items + m, down)
 
     def wait_along(m):
         for side in range(2):
-            there = ag.at[NC + side * items + m]
+            there = ag.at[side * items + m]
             pltpu.make_async_copy(there, there, ag_recv.at[side * items + m]).wait()
 
     for c in range(NC):
-        plus(c, c)
-        minus(c, c)
+        plus(own.at[c], c)
+        minus(own.at[c], c)
 
     def choose(src, label, c, row):
-        blocks = [ag[src, pl.ds(b * rows, rows), :] for b in range(HELD)]
-        for j, to in enumerate((ex, right, left, across)):
-            want = pick_ref[to * n_ex + row * NX + x]
+        blocks = [src[pl.ds(b * rows, rows), :] for b in range(HELD)]
+        for j, word in enumerate(words):
+            want = jnp.bitwise_and(jnp.right_shift(word, 2 * row), HELD - 1)
             v = blocks[HELD - 1]
             for b in range(HELD - 1):
                 v = jnp.where(want == b, blocks[b], v)
@@ -166,7 +273,7 @@
         return right if c % 2 == 0 else left
 
     for c in range(NC):
-        choose(c, 0, c, y)
+        choose(own.at[c], 0, c, y)
     for c in range(NC):
         push(0, c, own_via(c))
 
@@ -191,14 +298,14 @@
 
         @pl.when(m < items - NC)
         def _():
-            plus(NC + m, m + NC)
+            plus(ag.at[m], m + NC)
 
         @pl.when((m < regular - NC) | (m >= regular - NC // 2))
         def _():
-            minus(NC + items + m, jnp.where(m < regular - NC, m + NC, m + NC // 2))
-
-        choose(NC + m, a, c, (y + ny - k) % ny)
-        choose(NC + items + m, b, c, (y + k) % ny)
+            minus(ag.at[items + m], jnp.where(m < regular - NC, m + NC, m + NC // 2))
+
+        choose(ag.at[m], a, c, (y + ny - k) % ny)
+        choose(ag.at[items + m], b, c, (y + k) % ny)
         push(a, c, right)
         push(b, c, left)
 
@@ -237,7 +344,7 @@
         m = regular + t
         wait_along(m)
         for side, (c, _) in enumerate(spot):
-            choose(NC + side * items + m, last, c, opposite)
+            choose(ag.at[side * items + m], last, c, opposite)
         for c, via in spot:
             push(last, c, via)
         if t == 0:
@@ -245,12 +352,13 @@
         else:
             for c, via in spots[t - 1]:
                 relay(last, c, via)
-        multiply_step(m - LAG)
+        if t < len(spots) - 1:
+            multiply_step(m - LAG)
+    for m in range(regular + len(spots) - 1 - LAG, regular):
+        multiply_step(m)
+    reduce_pair(half - 2)
     for c, via in spots[-1]:
         relay(last, c, via)
-    for m in range(regular + len(spots) - LAG, regular):
-        multiply_step(m)
-    reduce_pair(half - 2)
     for spot in spots:
         for c, _ in spot:
             multiply(last, c, 1)
@@ -291,8 +399,7 @@
         v = total[pl.ds(label * NX + off, 1), :]
         out_ref[0, pl.ds(p, 1), :] = jnp.where(block >= 0, v, jnp.zeros_like(v))
 
-    sent = ag.at[pl.ds(NC, 2 * items)]
-    pltpu.make_async_copy(sent, sent, ag_send).wait()
+    pltpu.make_async_copy(ag, ag, ag_send).wait()
     pltpu.make_async_copy(stage, stage, x_send).wait()
     pltpu.make_async_copy(fwd, fwd, fwd_send).wait()
     pltpu.make_async_copy(recv_pair, recv_pair, pair_send).wait()
@@ -313,16 +420,29 @@
     half = ny // 2
     items = NC * (half - 1) + NC // 2
 
-    wanted = pair_blocks.reshape(n_ex, slots)
-    hit = (wanted[:, :, None] // HELD == jnp.arange(n_ex)[None, None, :]) & (wanted[:, :, None] >= 0)
-    pick = jnp.sum(jnp.where(hit, wanted[:, :, None] % HELD, 0), axis=1).astype(jnp.int32).reshape(-1)
-
-    own = precondition(query_grads[:, 0, :], in_precond[0], out_precond[0])
-    own = own.reshape(held_rows, NC, width).transpose(1, 0, 2)
+    query = query_grads.reshape(held_rows, features)
     train = train_grads.reshape(train_rows, features)
 
     bf16, f32 = jnp.bfloat16, jnp.float32
     dma = pltpu.SemaphoreType.DMA
+    whole = 67043328
+    own, words = pl.pallas_call(
+        functools.partial(prepare_kernel, n_ex, slots),
+        out_shape=(
+            jax.ShapeDtypeStruct((NC, held_rows, width), bf16),
+            jax.ShapeDtypeStruct((NX,), jnp.int32),
+        ),
+        in_specs=[
+            pl.BlockSpec(memory_space=pltpu.SMEM),
+            pl.BlockSpec(memory_space=pltpu.VMEM),
+            pl.BlockSpec(memory_space=pltpu.VMEM),
+            pl.BlockSpec(memory_space=pltpu.VMEM),
+        ],
+        out_specs=(pl.BlockSpec(memory_space=pltpu.VMEM), pl.BlockSpec(memory_space=pltpu.SMEM)),
+        scratch_shapes=[pltpu.VMEM((held_rows * features // LANES, LANES), f32)],
+        compiler_params=pltpu.CompilerParams(vmem_limit_bytes=whole),
+        name="prepare",
+    )(pair_blocks, query, in_precond, out_precond)
     return pl.pallas_call(
         functools.partial(kernel, n_ex, layers, slots),
         out_shape=jax.ShapeDtypeStruct((1, slots, train_rows), f32),
@@ -334,7 +454,8 @@
         ],
         out_specs=pl.BlockSpec(memory_space=pltpu.VMEM),
         scratch_shapes=[
-            pltpu.VMEM((NC + 2 * items, held_rows, width), bf16),
+            pltpu.VMEM((NC, held_rows, width), bf16),
+            pltpu.VMEM((2 * items, held_rows, width), bf16),
             pltpu.VMEM((NC, ny, NX * rows, width), bf16),
             pltpu.VMEM((NC, ny, 3, rows, width), bf16),
             pltpu.VMEM((NC, ny, rows, width), bf16),
@@ -358,10 +479,10 @@
             dma((2,)),
         ],
         compiler_params=pltpu.CompilerParams(
-            collective_id=0, has_side_effects=True, vmem_limit_bytes=48 * 1024 * 1024
+            collective_id=0, has_side_effects=True, vmem_limit_bytes=whole
         ),
         name="tiles",
-    )(pick, pair_blocks, own, train)
+    )(words, pair_blocks, own, train)
 
 
 def solution(mesh):

time: 86.4 us -> 80 us (0.926)
  local copies, waits for them, and re-layouts: 6.51 us -> 1.42 us
  matrix products: 4.76 us -> 0 us
  Pallas kernels: 74.3 us -> 78.4 us
    pallas_call x0 -> x1, Pallas kernels: none -> 4.83 us  [shards(): pl.pallas_call(functools.partial(prepare_kernel, n_ex, slots), out_shape=...]
    dot_general x2 -> x0, matrix products: 4.76 us -> none  [the longest x1 3.52 us: precondition(): jnp.einsum('roi,ik->rok', left_side, in_precond, precision=lax.Precision....]
    reshape x2 -> x0, local copies, waits for them, and re-layouts: 2.13 us -> none  [the longest x1 2.06 us: precondition(): blocks.astype(jnp.float32)]
    unnamed x9 -> x1, local copies, waits for them, and re-layouts: 2.82 us -> 1.42 us
where the time goes in v2:
time: 80 us; the launch traced here: 79.8 us
  Pallas kernels  78.4 us (98%)
  local copies, waits for them, and re-layouts  1.42 us (2%)
    pallas_call x1, Pallas kernels, shards(): pl.pallas_call(functools.partial(kernel, n_ex, layers, slots), out_shape=...  73.5 us
    pallas_call x1, Pallas kernels, shards(): pl.pallas_call(functools.partial(prepare_kernel, n_ex, slots), out_shape=...  4.83 us

profile of v2, /device:TPU:1, one launch (start us, length us, event | category | flops | bytes accessed | tf_op | source)
XLA Modules:
  0.0 79.8 jit_solution(789049859433114457)
XLA Ops:
  0.0 4.8 %prepare.1 = (bf16[4,64,1024]{2,1,0:T(8,128)(2,1)}, s32[4]{0:T(128)}) custom-call(s32[768]{0:T(1024)} %pair_ref.3, bf16[64,4096]{1,0:T(8,128)(2,1)} %bitcast.3, f32[1,64,64]{2,1,0:T(8,128)} %in_ref.1, f32[1,64,64]{2,1,0:T(8,128)} %out_pre_ref.1), custom_call_target="tpu_custom_call" | custom-call | tf_op jit(solution)/shard_map/prepare/pallas_call | solution.py:429
  4.8 73.5 %tiles.1 = f32[1,24,512]{2,1,0:T(8,128)} custom-call(s32[4]{0:T(128)} %get-tuple-element.7.words_ref, s32[768]{0:T(1024)} %pair_ref.3, bf16[4,64,1024]{2,1,0:T(8,128)(2,1)} %get-tuple-element.8.own_hbm, bf16[512,4096]{1,0:T(8,128)(2,1)} %bitcast.2), custom_call_target="tpu_custom_call" | custom-call | tf_op jit(solution)/shard_map/tiles/pallas_call | solution.py:446
  78.4 1.4 %copy.7 = f32[1,24,512]{2,1,0:T(8,128)} copy(f32[1,24,512]{2,1,0:T(8,128)} %tiles.1) | data formatting | bytes 98304

commit v3 on v2

--- a/solution.py
+++ b/solution.py
@@ -78,7 +78,7 @@
     return (high + low).astype(jnp.bfloat16)
 
 
-def prepare(query_v, left_factor, right_factor, mid):
+def prepare(query_v, left_factor, right_factor, mid, turned):
     held, features = query_v.shape
     pairs = features // LANES
     n = LANES // 2
@@ -99,8 +99,8 @@
 
     def apart(t, z):
         even, odd = z[:pairs], z[pairs:]
-        mid[pl.ds(2 * t, pairs, stride=held), :] = jnp.where(low, even, pltpu.roll(odd, n, 1))
-        mid[pl.ds(2 * t + 1, pairs, stride=held), :] = jnp.where(low, pltpu.roll(even, n, 1), odd)
+        turned[pl.ds(2 * t * pairs, pairs), :] = jnp.where(low, even, pltpu.roll(odd, n, 1))
+        turned[pl.ds((2 * t + 1) * pairs, pairs), :] = jnp.where(low, pltpu.roll(even, n, 1), odd)
 
     for t in range(0, held // 2, 2):
         (h0, l0), (h1, l1) = side_by_side(t), side_by_side(t + 1)
@@ -111,27 +111,27 @@
         apart(t + 1, z[:, LANES:])
 
 
-def finish(mid, own):
+def finish(turned, own):
     chunks, held, width = own.shape
     each = width // LANES
-    for d in range(chunks * each):
-        own[d // each, :, pl.ds(d % each * LANES, LANES)] = mid[pl.ds(d * held, held), :].astype(jnp.bfloat16)
-
-
-def prepare_kernel(n_ex, slots, pair_ref, query_ref, in_ref, out_pre_ref, own_ref, words_ref, mid):
+    pairs = chunks * each
+    for d in range(pairs):
+        v = turned[pl.ds(d, held, stride=pairs), :]
+        own[d // each, :, pl.ds(d % each * LANES, LANES)] = v.astype(jnp.bfloat16)
+
+
+def words_kernel(slots, pair_ref, words_ref):
     ex = lax.axis_index("ex")
     y, x = ex // NX, ex % NX
     to = [y * NX + (x + d) % NX for d in (0, 1, 3, 2)]
     for j, word in enumerate(wanted_words(pair_ref, to, slots, x)):
         words_ref[j] = word
-    prepare(query_ref, spread_out(out_pre_ref[0]), spread_in(in_ref[0]), mid)
-    finish(mid, own_ref)
 
 
 def kernel(
     n_ex, layers, slots,
-    words_ref, pair_ref, own_hbm, train_hbm, out_ref,
-    own, ag, recv, stage, fwd, train_v, acc, send_pair, recv_pair, send_one, recv_one, total,
+    words_ref, pair_ref, query_ref, in_ref, out_pre_ref, train_hbm, out_ref,
+    mid, turned, made, own, ag, recv, stage, fwd, train_v, acc, send_pair, recv_pair, send_one, recv_one, total,
     load_sem, ag_send, ag_recv, x_send, x_recv, fwd_send, fwd_recv, pair_send, one_send, pair_recv, one_recv,
 ):
     ny = n_ex // NX
@@ -151,13 +151,12 @@
     across = y * NX + (x + 2) % NX
 
     def load_own():
-        return pltpu.make_async_copy(own_hbm, own, load_sem.at[NC])
+        return pltpu.make_async_copy(made, own, load_sem.at[NC])
 
     def load_train(c):
         width = train_v.shape[2]
         return pltpu.make_async_copy(train_hbm.at[:, pl.ds(c * width, width)], train_v.at[c], load_sem.at[c])
 
-    load_own().start()
     for c in range(NC):
         load_train(c).start()
 
@@ -170,6 +169,9 @@
         pl.semaphore_signal(barrier, inc=1, device_id={"layer": (lay + r) % layers}, device_id_type=MESH)
 
     acc[...] = jnp.zeros_like(acc)
+    prepare(query_ref, spread_out(out_pre_ref[0]), spread_in(in_ref[0]), mid, turned)
+    finish(turned, made)
+    load_own().start()
     load_own().wait()
     pl.semaphore_wait(barrier, 4 + layers - 1)
     words = [words_ref[j] for j in range(NX)]
@@ -426,34 +428,30 @@
     bf16, f32 = jnp.bfloat16, jnp.float32
     dma = pltpu.SemaphoreType.DMA
     whole = 67043328
-    own, words = pl.pallas_call(
-        functools.partial(prepare_kernel, n_ex, slots),
-        out_shape=(
-            jax.ShapeDtypeStruct((NC, held_rows, width), bf16),
-            jax.ShapeDtypeStruct((NX,), jnp.int32),
-        ),
-        in_specs=[
-            pl.BlockSpec(memory_space=pltpu.SMEM),
-            pl.BlockSpec(memory_space=pltpu.VMEM),
-            pl.BlockSpec(memory_space=pltpu.VMEM),
-            pl.BlockSpec(memory_space=pltpu.VMEM),
-        ],
-        out_specs=(pl.BlockSpec(memory_space=pltpu.VMEM), pl.BlockSpec(memory_space=pltpu.SMEM)),
-        scratch_shapes=[pltpu.VMEM((held_rows * features // LANES, LANES), f32)],
-        compiler_params=pltpu.CompilerParams(vmem_limit_bytes=whole),
-        name="prepare",
-    )(pair_blocks, query, in_precond, out_precond)
+    smem = pl.BlockSpec(memory_space=pltpu.SMEM)
+    words = pl.pallas_call(
+        functools.partial(words_kernel, slots),
+        out_shape=jax.ShapeDtypeStruct((NX,), jnp.int32),
+        in_specs=[smem],
+        out_specs=smem,
+        name="words",
+    )(pair_blocks)
     return pl.pallas_call(
         functools.partial(kernel, n_ex, layers, slots),
         out_shape=jax.ShapeDtypeStruct((1, slots, train_rows), f32),
         in_specs=[
-            pl.BlockSpec(memory_space=pltpu.SMEM),
-            pl.BlockSpec(memory_space=pltpu.SMEM),
-            pl.BlockSpec(memory_space=pl.ANY),
+            smem,
+            smem,
+            pl.BlockSpec(memory_space=pltpu.VMEM),
+            pl.BlockSpec(memory_space=pltpu.VMEM),
+            pl.BlockSpec(memory_space=pltpu.VMEM),
             pl.BlockSpec(memory_space=pl.ANY),
         ],
         out_specs=pl.BlockSpec(memory_space=pltpu.VMEM),
         scratch_shapes=[
+            pltpu.VMEM((held_rows * features // LANES, LANES), f32),
+            pltpu.VMEM((held_rows * features // LANES, LANES), f32),
+            pltpu.VMEM((NC, held_rows, width), bf16),
             pltpu.VMEM((NC, held_rows, width), bf16),
             pltpu.VMEM((2 * items, held_rows, width), bf16),
             pltpu.VMEM((NC, ny, NX * rows, width), bf16),
@@ -482,7 +480,7 @@
             collective_id=0, has_side_effects=True, vmem_limit_bytes=whole
         ),
         name="tiles",
-    )(words, pair_blocks, own, train)
+    )(words, pair_blocks, query, in_precond, out_precond, train)
 
 
 def solution(mesh):

time: 80 us -> 77.2 us (0.965)
  Pallas kernels: 78.4 us -> 75.5 us
    pallas_call x1, Pallas kernels: 4.83 us -> 1.77 us  [shards(): pl.pallas_call(functools.partial(words_kernel, slots), out_shape=jax.Shap...]
where the time goes in v3:
time: 77.2 us; the launch traced here: 77 us
  Pallas kernels  75.5 us (98%)
  local copies, waits for them, and re-layouts  1.42 us (2%)
    pallas_call x1, Pallas kernels, shards(): pl.pallas_call(functools.partial(kernel, n_ex, layers, slots), out_shape=...  73.8 us
    pallas_call x1, Pallas kernels, shards(): pl.pallas_call(functools.partial(words_kernel, slots), out_shape=jax.Shap...  1.77 us

profile of v3, /device:TPU:1, one launch (start us, length us, event | category | flops | bytes accessed | tf_op | source)
XLA Modules:
  0.0 77.0 jit_solution(6404321142878109698)
XLA Ops:
  0.0 1.8 %words.1.words_ref = s32[4]{0:T(128)} custom-call(s32[768]{0:T(1024)} %pair_ref.3), custom_call_target="tpu_custom_call" | custom-call | tf_op jit(solution)/shard_map/words/pallas_call | solution.py:432
  1.8 73.8 %tiles.1 = f32[1,24,512]{2,1,0:T(8,128)} custom-call(s32[4]{0:T(128)} %words.1.words_ref, s32[768]{0:T(1024)} %pair_ref.3, bf16[64,4096]{1,0:T(8,128)(2,1)} %bitcast.3, f32[1,64,64]{2,1,0:T(8,128)} %in_ref.1, f32[1,64,64]{2,1,0:T(8,128)} %out_pre_ref.1, bf16[512,4096]{1,0:T(8,128)(2,1)} %bitcast.2), custom_call_target="tpu_custom_call" | custom-call | tf_op jit(solution)/shard_map/tiles/pallas_call | solution.py:439
  75.6 1.4 %copy.7 = f32[1,24,512]{2,1,0:T(8,128)} copy(f32[1,24,512]{2,1,0:T(8,128)} %tiles.1) | data formatting | bytes 98304
